TPU v7x, 128 devices: a whole 4x4x4 slice. The times are simulated.
128 devices in a mesh: section: 8 (over y, core), fsdp: 16 (over x, z).
Axes of the slice: x: 4, y: 4, z: 4, core: 2. Of those that a mesh axis runs over, the one named last changes fastest.
Arguments:
- layer_input: bfloat16 [8, 8192, 2048], P('section', 'fsdp'), may hold values from -6 to 6
- resid_grad: bfloat16 [8, 8192, 2048], P('section', 'fsdp'), may hold values from -6 to 6
- qkv_grad: bfloat16 [8, 8192, 3072], P('section', 'fsdp'), may hold values from -6 to 6
- prev_input: bfloat16 [8, 8192, 2048], P('section', 'fsdp'), may hold values from -6 to 6
- prev_qkv_grad: bfloat16 [8, 8192, 3072], P('section', 'fsdp'), may hold values from -0.059814453 to 0.059814453
- qkv_weight: bfloat16 [8, 2048, 3072], P('section', 'fsdp'), may hold values from -0.125 to 0.125
- norm_gain: float32 [8, 2048], P('section'), may hold values from 0.1 to 1.9
Outputs:
- upstream_grad: bfloat16 [8, 8192, 2048], P('section', 'fsdp')
- weight_grad: float32 [8, 2048, 3072], P('section', 'fsdp')
- gain_grad: float32 [8, 2048], P('section')
All inputs are finite; a program needn't handle non-finite values.
Results may differ from a plain program's by a relative error of at most 0.018.
Values may be sent and summed in bfloat16 or wider, within the bound.
A program may use at most 128 MiB of HBM per device.

v0:
```python
import jax
import jax.numpy as jnp
from jax import lax
from jax.sharding import PartitionSpec as P

EPS = 1e-05


def from_behind(block, axis, distance):
    devices = range(lax.axis_size(axis))
    route = [(i - distance, i) for i in devices if i - distance in devices]
    return lax.ppermute(block, axis, route)


def row_scale(rows):
    values = rows.astype(jnp.float32)
    return lax.rsqrt(jnp.mean(values * values, axis=-1, keepdims=True) + EPS)


def transpose_product(grads, piece):
    return lax.dot_general(
        grads, piece, (((1,), (1,)), ((), ())), preferred_element_type=jnp.float32
    )


def local(layer_input, resid_grad, qkv_grad, prev_input, prev_qkv_grad, qkv_weight, norm_gain):
    rows_now = layer_input[0]
    grads_now = qkv_grad[0]
    rows_prev = prev_input[0]
    grads_prev = prev_qkv_grad[0]
    weight_rows = qkv_weight[0]
    gain = norm_gain[0]
    owned = weight_rows.shape[0]
    prev_scale = row_scale(rows_prev)
    prev_normed = (rows_prev.astype(jnp.float32) * prev_scale * gain[None, :]).astype(jnp.bfloat16)
    direction = transpose_product(
        grads_now, lax.all_gather(weight_rows, "fsdp", axis=0, tiled=True)
    )
    scale = row_scale(rows_now)
    values = rows_now.astype(jnp.float32)
    gained = gain[None, :] * direction
    inner = jnp.mean(gained * values, axis=-1, keepdims=True)
    local_grad = (
        resid_grad[0].astype(jnp.float32) + scale * gained - values * scale * scale * scale * inner
    ).astype(jnp.bfloat16)
    upstream_grad = from_behind(local_grad, "section", -1)
    weight_grad = lax.psum_scatter(
        lax.dot_general(
            prev_normed, grads_prev, (((0,), (0,)), ((), ())), preferred_element_type=jnp.float32
        ).astype(jnp.bfloat16),
        "fsdp",
        scatter_dimension=0,
        tiled=True,
    ).astype(jnp.float32)
    owned_gain = lax.dynamic_slice_in_dim(gain, lax.axis_index("fsdp") * owned, owned, 0)
    gain_part = jnp.sum(weight_rows.astype(jnp.float32) * weight_grad, axis=1) / owned_gain
    gain_grad = lax.all_gather(gain_part, "fsdp", axis=0, tiled=True)
    return (upstream_grad[None], weight_grad[None], gain_grad[None])


def solution(mesh):
    placed = (
        P("section", "fsdp", None),
        P("section", "fsdp", None),
        P("section", "fsdp", None),
        P("section", "fsdp", None),
        P("section", "fsdp", None),
        P("section", "fsdp", None),
        P("section", None),
    )
    return jax.shard_map(
        local,
        mesh=mesh,
        in_specs=placed,
        out_specs=(P("section", "fsdp", None), P("section", "fsdp", None), P("section", None)),
        check_vma=False,
    )
```

profile of v0, /device:TPU:0, one launch (start us, length us, event | category | flops | bytes accessed | tf_op | source)
XLA Modules:
  0.0 234.6 jit_solution(13687583729323604503)
XLA Ops:
  7.2 0.0 copy-start
  7.2 0.0 all-gather.4.cloned.1.call-start
  7.2 0.7 all-gather.4.cloned.1.call-update
  7.9 0.0 reduce-scatter.2.cloned.1.call-start
  8.0 2.2 fusion.2
  10.2 0.0 copy-done
  10.2 11.6 %convolution_convert_fusion = bf16[2048,3072]{1,0:T(8,128)(2,1)} fusion(bf16[1,512,3072]{2,1,0:T(8,128)(2,1)S(1)} %copy-done, bf16[1,512,2048]{2,1,0:T(8,128)(2,1)} %param.10, f32[2048]{0:T(1024)} %bitcast.39, f32[512]{0:T(512)S(1)} %add_rsqrt_fusion), kind=kOutput, calls=%fused_computation.2 | convolution fusion | flops 6452936704 | bytes 17836032 | tf_op jit(solution)/shard_map/dot_general | solution.py:48
  21.8 0.0 copy-start.3
  21.8 0.0 reduce-scatter.2.cloned.1.call-update
  21.8 81.0 %all-gather.4.cloned.1.call-done = bf16[1,2048,3072]{2,1,0:T(8,128)(2,1)} async-done(((bf16[1,128,3072]{2,1,0:T(8,128)(2,1)}), bf16[1,2048,3072]{2,1,0:T(8,128)(2,1)}) %all-gather.4.cloned.1.call-update) | async-done | bytes 12582928 | tf_op jit(solution)/shard_map/all_gather | solution.py:37
  102.8 0.0 copy-done.3
  102.8 0.0 copy-start.1
  102.8 0.0 copy-start.2
  102.9 11.3 %fusion.5 = (f32[512]{0:T(512)S(1)}, f32[512]{0:T(512)S(1)}, f32[512,2048]{1,0:T(8,128)S(1)}) fusion(bf16[1,512,2048]{2,1,0:T(8,128)(2,1)} %param.7, f32[2048]{0:T(1024)S(1)} %bitcast.40, bf16[1,2048,3072]{2,1,0:T(8,128)(2,1)} %all-gather.4.cloned.1.call-done, bf16[1,512,3072]{2,1,0:T(8,128)(2,1)} %param.9), kind=kOutput, calls=%fused_computation.11 | convolution fusion | flops 6448741376 | bytes 22032384 | tf_op jit(solution)/shard_map/dot_general | solution.py:21
  114.2 0.0 copy-done.1
  114.2 0.0 copy-done.2
  114.2 3.1 %fusion.10 = bf16[512,2048]{1,0:T(8,128)(2,1)} fusion(f32[512,2048]{1,0:T(8,128)S(1)} %get-tuple-element.5, bf16[1,512,2048]{2,1,0:T(8,128)(2,1)S(1)} %copy-done.2, bf16[1,512,2048]{2,1,0:T(8,128)(2,1)S(1)} %copy-done.1, f32[512]{0:T(512)S(1)} %get-tuple-element.7, f32[2048]{0:T(1024)S(1)} %bitcast.41, f32[512]{0:T(512)S(1)} %get-tuple-element.6), kind=kLoop, calls=%fused_computation.16 | loop fusion | flops 11534336 | bytes 10498048 | tf_op jit(solution)/shard_map/convert_element_type | solution.py:45
  117.3 1.3 collective-permute-start
  118.6 82.1 %reduce-scatter.2.cloned.1.call-done = bf16[128,3072]{1,0:T(8,128)(2,1)} async-done(((bf16[2048,3072]{1,0:T(8,128)(2,1)}), bf16[128,3072]{1,0:T(8,128)(2,1)}) %reduce-scatter.2.cloned.1.call-update) | async-done | bytes 786448 | tf_op jit(solution)/shard_map/reduce_scatter | solution.py:47
  200.6 1.7 fusion.18
  202.3 19.3 %all-gather.1 = f32[16,1,128]{2,1,0:T(1,128)S(1)} all-gather(f32[1,1,128]{2,1,0:T(1,128)S(1)} %fusion.19), channel_id=1, replica_groups=mesh['section'=8,'fsdp'=16] {'fsdp'}, dimensions={0}, use_global_device_ids=true | all-gather | bytes 8704 | tf_op jit(solution)/shard_map/all_gather | solution.py:57
  221.6 2.4 %convert_bitcast_fusion = f32[1,128,3072]{2,1,0:T(8,128)} fusion(bf16[128,3072]{1,0:T(8,128)(2,1)} %reduce-scatter.2.cloned.1.call-done), kind=kLoop, calls=%fused_computation.25 | loop fusion | flops 393216 | bytes 2359296 | tf_op jit(solution)/shard_map/broadcast_in_dim | solution.py:58
  224.0 0.0 collective-permute-done
  224.0 3.2 %copy.12 = bf16[1,512,2048]{2,1,0:T(8,128)(2,1)} copy(bf16[1,512,2048]{2,1,0:T(8,128)(2,1)} %bitcast.6) | data formatting | bytes 4194304
  227.2 0.6 copy.13
  (3 shorter events, 0.0 us)
Async XLA Ops:
  7.2 3.0 %copy-start = (bf16[1,512,3072]{2,1,0:T(8,128)(2,1)S(1)}, bf16[1,512,3072]{2,1,0:T(8,128)(2,1)}, u32[]{:S(2)}) copy-start(bf16[1,512,3072]{2,1,0:T(8,128)(2,1)} %param.11) | copy-start | bytes 9437188
  7.2 95.7 %all-gather.4.cloned.1.call-start = ((), (), s32[]{:S(2)}) async-start(), calls=%async_computation.2 | async-start | bytes 13369344 | tf_op jit(solution)/shard_map/all_gather | solution.py:37
  7.9 192.7 %reduce-scatter.2.cloned.1.call-start = ((), (), s32[]{:S(2)}) async-start(), calls=%async_computation.1 | async-start | bytes 13369344 | tf_op jit(solution)/shard_map/reduce_scatter | solution.py:47
  21.8 81.1 %copy-start.3 = (f32[1,2048]{1,0:T(1,128)S(1)}, f32[1,2048]{1,0:T(1,128)}, u32[]{:S(2)}) copy-start(f32[1,2048]{1,0:T(1,128)} %param.13) | copy-start | bytes 24580
  102.8 11.3 %copy-start.1 = (bf16[1,512,2048]{2,1,0:T(8,128)(2,1)S(1)}, bf16[1,512,2048]{2,1,0:T(8,128)(2,1)}, u32[]{:S(2)}) copy-start(bf16[1,512,2048]{2,1,0:T(8,128)(2,1)} %param.7) | copy-start | bytes 6291460
  102.8 11.3 %copy-start.2 = (bf16[1,512,2048]{2,1,0:T(8,128)(2,1)S(1)}, bf16[1,512,2048]{2,1,0:T(8,128)(2,1)}, u32[]{:S(2)}) copy-start(bf16[1,512,2048]{2,1,0:T(8,128)(2,1)} %param.8) | copy-start | bytes 6291460
  117.3 106.7 %collective-permute-start = (bf16[512,2048]{1,0:T(8,128)(2,1)}, bf16[512,2048]{1,0:T(8,128)(2,1)}, u32[]{:S(2)}, u32[]{:S(2)}) collective-permute-start(bf16[512,2048]{1,0:T(8,128)(2,1)} %fusion.10), channel_id=1, source_target_pairs={{16,0},{32,16},{48,32},{64,48},{80,64},{96,80},{112,96},{17,1},{33... | collective-permute-start | bytes 6291464 | tf_op jit(solution)/shard_map/ppermute | solution.py:12
Sparse Core Ops, SparseCore 0:
  10.2 92.5 all-gather.3
  106.3 94.3 reduce-scatter.1
where the time goes:
time: 235 us
  waiting for transfers between devices  164 us (70%)
  matrix products  22.9 us (10%)
  blocking collectives  19.3 us (8%)
  between operations  14.1 us (6%)
  other arithmetic  9.45 us (4%)
  local copies, waits for them, and re-layouts  3.78 us (2%)
    reduce_scatter x1, waiting for transfers between devices, local(): lax.psum_scatter(lax.dot_general(prev_normed, grads_prev, (((0,), (0,)),...  82.1 us
    all_gather x1, waiting for transfers between devices, local(): lax.all_gather(weight_rows, 'fsdp', axis=0, tiled=True)  81 us
    all_gather x1, blocking collectives, local(): gain_grad = lax.all_gather(gain_part, 'fsdp', axis=0, tiled=True)  19.3 us
    dot_general x1, matrix products, local(): lax.dot_general(prev_normed, grads_prev, (((0,), (0,)), ((), ())), prefer...  11.6 us
    dot_general x1, matrix products, transpose_product(): lax.dot_general(grads, piece, (((1,), (1,)), ((), ())), preferred_element...  11.3 us
  transfers between devices with their start and end apart: 3, of which 2 were waited for; matrix products, arithmetic and copies ran while one was open for 14% of the time, Pallas kernels for 0%

commit v1 on v0

--- a/solution.py
+++ b/solution.py
@@ -4,6 +4,27 @@
 from jax.sharding import PartitionSpec as P
 
 EPS = 1e-05
+
+
+def ring_gather(x, axis, dim):
+    size, place, extent = (lax.axis_size(axis), lax.axis_index(axis), x.shape[dim])
+    ahead = [(i, (i + 1) % size) for i in range(size)]
+    backward = [(i, (i - 1) % size) for i in range(size)]
+    out = jnp.zeros((*x.shape[:dim], size * extent, *x.shape[dim + 1 :]), x.dtype)
+    out = lax.dynamic_update_slice_in_dim(out, x, place * extent, axis=dim)
+    from_left = from_right = x
+    half = size // 2
+    for hop in range(1, half + 1):
+        from_left = lax.ppermute(from_left, axis, ahead)
+        out = lax.dynamic_update_slice_in_dim(
+            out, from_left, (place - hop) % size * extent, axis=dim
+        )
+        if hop < size - half:
+            from_right = lax.ppermute(from_right, axis, backward)
+            out = lax.dynamic_update_slice_in_dim(
+                out, from_right, (place + hop) % size * extent, axis=dim
+            )
+    return out
 
 
 def from_behind(block, axis, distance):
@@ -54,7 +75,7 @@
     ).astype(jnp.float32)
     owned_gain = lax.dynamic_slice_in_dim(gain, lax.axis_index("fsdp") * owned, owned, 0)
     gain_part = jnp.sum(weight_rows.astype(jnp.float32) * weight_grad, axis=1) / owned_gain
-    gain_grad = lax.all_gather(gain_part, "fsdp", axis=0, tiled=True)
+    gain_grad = ring_gather(gain_part, "fsdp", 0)
     return (upstream_grad[None], weight_grad[None], gain_grad[None])
 
 

time: 235 us -> 269 us (1.14)
  starting transfers between devices: 1.36 us -> 38.9 us
  blocking collectives: 19.3 us -> 0 us
  waiting for transfers between devices: 164 us -> 179 us
    ppermute x0 -> x15, starting transfers between devices: none -> 37.6 us  [the longest x7 36.5 us: ring_gather(): from_right = lax.ppermute(from_right, axis, backward)]
    all_gather x1 -> x0, blocking collectives: 19.3 us -> none  [local(): gain_grad = lax.all_gather(gain_part, 'fsdp', axis=0, tiled=True)]
    ppermute x0 -> x15, waiting for transfers between devices: none -> 15.8 us  [the longest x8 15.8 us: ring_gather(): from_left = lax.ppermute(from_left, axis, ahead)]
  transfers between devices with their start and end apart: 3 -> 18, of which waited for: 2 -> 9; matrix products, arithmetic and copies ran while one was open for 14% -> 12% of each run, Pallas kernels for 0% -> 0%
where the time goes in v1:
time: 269 us; the launch traced here: 268 us
  waiting for transfers between devices  179 us (67%)
  starting transfers between devices  38.9 us (14%)
  matrix products  22.9 us (9%)
  between operations  14.4 us (5%)
  other arithmetic  9.46 us (4%)
  local copies, waits for them, and re-layouts  3.31 us (1%)
    reduce_scatter x1, waiting for transfers between devices, local(): lax.psum_scatter(lax.dot_general(prev_normed, grads_prev, (((0,), (0,)),...  82 us
    all_gather x1, waiting for transfers between devices, local(): lax.all_gather(weight_rows, 'fsdp', axis=0, tiled=True)  80.8 us
    ppermute x7, starting transfers between devices, ring_gather(): from_right = lax.ppermute(from_right, axis, backward)  36.5 us
    ppermute x8, waiting for transfers between devices, ring_gather(): from_left = lax.ppermute(from_left, axis, ahead)  15.8 us
    dot_general x1, matrix products, local(): lax.dot_general(prev_normed, grads_prev, (((0,), (0,)), ((), ())), prefer...  11.6 us
    dot_general x1, matrix products, transpose_product(): lax.dot_general(grads, piece, (((1,), (1,)), ((), ())), preferred_element...  11.3 us
  transfers between devices with their start and end apart: 18, of which 9 were waited for; matrix products, arithmetic and copies ran while one was open for 12% of the time, Pallas kernels for 0%

profile of v1, /device:TPU:0, one launch (start us, length us, event | category | flops | bytes accessed | tf_op | source)
XLA Modules:
  0.0 268.3 jit_solution(15597129713506685397)
XLA Ops:
  7.2 0.0 copy-start
  7.2 0.0 all-gather.3.cloned.1.call-start
  7.2 0.7 all-gather.3.cloned.1.call-update
  7.9 0.0 reduce-scatter.2.cloned.1.call-start
  8.0 2.2 fusion.2
  10.2 0.0 copy-done
  10.2 11.6 %convolution_convert_fusion = bf16[2048,3072]{1,0:T(8,128)(2,1)} fusion(bf16[1,512,3072]{2,1,0:T(8,128)(2,1)S(1)} %copy-done, bf16[1,512,2048]{2,1,0:T(8,128)(2,1)} %param.10, f32[2048]{0:T(1024)} %bitcast.65, f32[512]{0:T(512)S(1)} %add_rsqrt_fusion), kind=kOutput, calls=%fused_computation.2 | convolution fusion | flops 6452936704 | bytes 17836032 | tf_op jit(solution)/shard_map/dot_general | solution.py:69
  21.8 0.0 reduce-scatter.2.cloned.1.call-update
  22.1 80.8 %all-gather.3.cloned.1.call-done = bf16[1,2048,3072]{2,1,0:T(8,128)(2,1)} async-done(((bf16[1,128,3072]{2,1,0:T(8,128)(2,1)}), bf16[1,2048,3072]{2,1,0:T(8,128)(2,1)}) %all-gather.3.cloned.1.call-update) | async-done | bytes 12582928 | tf_op jit(solution)/shard_map/all_gather | solution.py:58
  102.8 0.0 copy-done.3
  102.9 11.3 %fusion.5 = (f32[512]{0:T(512)S(1)}, f32[512]{0:T(512)S(1)}, f32[512,2048]{1,0:T(8,128)S(1)}) fusion(bf16[1,512,2048]{2,1,0:T(8,128)(2,1)} %param.7, f32[2048]{0:T(1024)S(1)} %bitcast.66, bf16[1,2048,3072]{2,1,0:T(8,128)(2,1)} %all-gather.3.cloned.1.call-done, bf16[1,512,3072]{2,1,0:T(8,128)(2,1)} %param.9), kind=kOutput, calls=%fused_computation.11 | convolution fusion | flops 6448741376 | bytes 22032384 | tf_op jit(solution)/shard_map/dot_general | solution.py:42
  114.2 3.1 %fusion.10 = bf16[512,2048]{1,0:T(8,128)(2,1)} fusion(f32[512,2048]{1,0:T(8,128)S(1)} %get-tuple-element.5, bf16[1,512,2048]{2,1,0:T(8,128)(2,1)S(1)} %copy-done.2, bf16[1,512,2048]{2,1,0:T(8,128)(2,1)S(1)} %copy-done.1, f32[512]{0:T(512)S(1)} %get-tuple-element.7, f32[2048]{0:T(1024)S(1)} %bitcast.67, f32[512]{0:T(512)S(1)} %get-tuple-element.6), kind=kLoop, calls=%fused_computation.16 | loop fusion | flops 11534336 | bytes 10498048 | tf_op jit(solution)/shard_map/convert_element_type | solution.py:66
  117.3 1.3 collective-permute-start
  118.6 82.0 %reduce-scatter.2.cloned.1.call-done = bf16[128,3072]{1,0:T(8,128)(2,1)} async-done(((bf16[2048,3072]{1,0:T(8,128)(2,1)}), bf16[128,3072]{1,0:T(8,128)(2,1)}) %reduce-scatter.2.cloned.1.call-update) | async-done | bytes 786448 | tf_op jit(solution)/shard_map/reduce_scatter | solution.py:68
  200.6 1.7 fusion.18
  202.3 0.9 collective-permute-start.1
  203.2 4.5 %collective-permute-start.2 = (f32[128]{0:T(128)S(1)}, f32[128]{0:T(128)S(1)}, u32[]{:S(2)}, u32[]{:S(2)}) collective-permute-start(f32[128]{0:T(128)S(1)} %bitcast_divide_fusion), channel_id=1, source_target_pairs={{0,15},{1,0},{2,1},{3,2},{4,3},{5,4},{6,5},{7,6},{8,7},{9,8},{10,9... | collective-permute-start | bytes 1544 | tf_op jit(solution)/shard_map/ppermute | solution.py:23
  207.7 2.4 convert_bitcast_fusion
  210.1 0.0 collective-permute-done.1
  210.2 0.1 collective-permute-start.3
  210.2 0.0 collective-permute-done.2
  210.3 5.3 %collective-permute-start.4 = (f32[128]{0:T(128)S(1)}, f32[128]{0:T(128)S(1)}, u32[]{:S(2)}, u32[]{:S(2)}) collective-permute-start(f32[128]{0:T(128)S(1)} %collective-permute-done.2), channel_id=1, source_target_pairs={{0,15},{1,0},{2,1},{3,2},{4,3},{5,4},{6,5},{7,6},{8,7},{9,8},{10,9... | collective-permute-start | bytes 1544 | tf_op jit(solution)/shard_map/ppermute | solution.py:23
  215.6 1.5 collective-permute-done.3
  217.1 0.0 collective-permute-start.5
  217.1 0.0 collective-permute-done.4
  217.1 5.3 %collective-permute-start.6 = (f32[128]{0:T(128)S(1)}, f32[128]{0:T(128)S(1)}, u32[]{:S(2)}, u32[]{:S(2)}) collective-permute-start(f32[128]{0:T(128)S(1)} %collective-permute-done.4), channel_id=1, source_target_pairs={{0,15},{1,0},{2,1},{3,2},{4,3},{5,4},{6,5},{7,6},{8,7},{9,8},{10,9... | collective-permute-start | bytes 1544 | tf_op jit(solution)/shard_map/ppermute | solution.py:23
  222.5 1.5 collective-permute-done.5
  223.9 0.0 collective-permute-start.7
  224.0 0.0 collective-permute-done.6
  224.0 5.3 %collective-permute-start.8 = (f32[128]{0:T(128)S(1)}, f32[128]{0:T(128)S(1)}, u32[]{:S(2)}, u32[]{:S(2)}) collective-permute-start(f32[128]{0:T(128)S(1)} %collective-permute-done.6), channel_id=1, source_target_pairs={{0,15},{1,0},{2,1},{3,2},{4,3},{5,4},{6,5},{7,6},{8,7},{9,8},{10,9... | collective-permute-start | bytes 1544 | tf_op jit(solution)/shard_map/ppermute | solution.py:23
  229.3 1.5 collective-permute-done.7
  230.8 0.0 collective-permute-start.9
  230.8 0.0 collective-permute-done.8
  230.8 5.3 %collective-permute-start.10 = (f32[128]{0:T(128)S(1)}, f32[128]{0:T(128)S(1)}, u32[]{:S(2)}, u32[]{:S(2)}) collective-permute-start(f32[128]{0:T(128)S(1)} %collective-permute-done.8), channel_id=1, source_target_pairs={{0,15},{1,0},{2,1},{3,2},{4,3},{5,4},{6,5},{7,6},{8,7},{9,8},{10,9... | collective-permute-start | bytes 1544 | tf_op jit(solution)/shard_map/ppermute | solution.py:23
  236.2 1.5 collective-permute-done.9
  237.7 0.0 collective-permute-start.11
  237.7 0.0 collective-permute-done.10
  237.7 5.3 %collective-permute-start.12 = (f32[128]{0:T(128)S(1)}, f32[128]{0:T(128)S(1)}, u32[]{:S(2)}, u32[]{:S(2)}) collective-permute-start(f32[128]{0:T(128)S(1)} %collective-permute-done.10), channel_id=1, source_target_pairs={{0,15},{1,0},{2,1},{3,2},{4,3},{5,4},{6,5},{7,6},{8,7},{9,8},{10,9... | collective-permute-start | bytes 1544 | tf_op jit(solution)/shard_map/ppermute | solution.py:23
  243.0 1.5 collective-permute-done.11
  244.5 0.0 collective-permute-start.13
  244.5 0.0 collective-permute-done.12
  244.5 5.3 %collective-permute-start.14 = (f32[128]{0:T(128)S(1)}, f32[128]{0:T(128)S(1)}, u32[]{:S(2)}, u32[]{:S(2)}) collective-permute-start(f32[128]{0:T(128)S(1)} %collective-permute-done.12), channel_id=1, source_target_pairs={{0,15},{1,0},{2,1},{3,2},{4,3},{5,4},{6,5},{7,6},{8,7},{9,8},{10,9... | collective-permute-start | bytes 1544 | tf_op jit(solution)/shard_map/ppermute | solution.py:23
  249.9 1.5 collective-permute-done.13
  251.4 0.0 collective-permute-start.15
  251.4 0.0 collective-permute-done.14
  251.4 6.8 %collective-permute-done.15 = f32[128]{0:T(128)S(1)} collective-permute-done((f32[128]{0:T(128)S(1)}, f32[128]{0:T(128)S(1)}, u32[]{:S(2)}, u32[]{:S(2)}) %collective-permute-start.15) | collective-permute-done | bytes 544 | tf_op jit(solution)/shard_map/ppermute | solution.py:18
  258.3 0.0 collective-permute-done
  258.3 3.2 %copy.27 = bf16[1,512,2048]{2,1,0:T(8,128)(2,1)} copy(bf16[1,512,2048]{2,1,0:T(8,128)(2,1)} %bitcast.6) | data formatting | bytes 4194304
  (27 shorter events, 0.2 us)
Async XLA Ops:
  7.2 3.0 %copy-start = (bf16[1,512,3072]{2,1,0:T(8,128)(2,1)S(1)}, bf16[1,512,3072]{2,1,0:T(8,128)(2,1)}, u32[]{:S(2)}) copy-start(bf16[1,512,3072]{2,1,0:T(8,128)(2,1)} %param.11) | copy-start | bytes 9437188
  7.2 95.7 %all-gather.3.cloned.1.call-start = ((), (), s32[]{:S(2)}) async-start(), calls=%async_computation.2 | async-start | bytes 13369344 | tf_op jit(solution)/shard_map/all_gather | solution.py:58
  7.9 192.7 %reduce-scatter.2.cloned.1.call-start = ((), (), s32[]{:S(2)}) async-start(), calls=%async_computation.1 | async-start | bytes 13369344 | tf_op jit(solution)/shard_map/reduce_scatter | solution.py:68
  21.8 81.1 %copy-start.3 = (f32[1,2048]{1,0:T(1,128)S(1)}, f32[1,2048]{1,0:T(1,128)}, u32[]{:S(2)}) copy-start(f32[1,2048]{1,0:T(1,128)} %param.13) | copy-start | bytes 24580
  102.8 11.3 %copy-start.1 = (bf16[1,512,2048]{2,1,0:T(8,128)(2,1)S(1)}, bf16[1,512,2048]{2,1,0:T(8,128)(2,1)}, u32[]{:S(2)}) copy-start(bf16[1,512,2048]{2,1,0:T(8,128)(2,1)} %param.7) | copy-start | bytes 6291460
  102.8 11.3 %copy-start.2 = (bf16[1,512,2048]{2,1,0:T(8,128)(2,1)S(1)}, bf16[1,512,2048]{2,1,0:T(8,128)(2,1)}, u32[]{:S(2)}) copy-start(bf16[1,512,2048]{2,1,0:T(8,128)(2,1)} %param.8) | copy-start | bytes 6291460
  117.3 141.0 %collective-permute-start = (bf16[512,2048]{1,0:T(8,128)(2,1)}, bf16[512,2048]{1,0:T(8,128)(2,1)}, u32[]{:S(2)}, u32[]{:S(2)}) collective-permute-start(bf16[512,2048]{1,0:T(8,128)(2,1)} %fusion.10), channel_id=1, source_target_pairs={{16,0},{32,16},{48,32},{64,48},{80,64},{96,80},{112,96},{17,1},{33... | collective-permute-start | bytes 6291464 | tf_op jit(solution)/shard_map/ppermute | solution.py:33
  202.3 7.9 %collective-permute-start.1 = (f32[128]{0:T(128)S(1)}, f32[128]{0:T(128)S(1)}, u32[]{:S(2)}, u32[]{:S(2)}) collective-permute-start(f32[128]{0:T(128)S(1)} %bitcast_divide_fusion), channel_id=1, source_target_pairs={{0,1},{1,2},{2,3},{3,4},{4,5},{5,6},{6,7},{7,8},{8,9},{9,10},{10,1... | collective-permute-start | bytes 1544 | tf_op jit(solution)/shard_map/ppermute | solution.py:18
  203.2 7.0 %collective-permute-start.2 = (f32[128]{0:T(128)S(1)}, f32[128]{0:T(128)S(1)}, u32[]{:S(2)}, u32[]{:S(2)}) collective-permute-start(f32[128]{0:T(128)S(1)} %bitcast_divide_fusion), channel_id=1, source_target_pairs={{0,15},{1,0},{2,1},{3,2},{4,3},{5,4},{6,5},{7,6},{8,7},{9,8},{10,9... | collective-permute-start | bytes 1544 | tf_op jit(solution)/shard_map/ppermute | solution.py:23
  210.2 6.9 %collective-permute-start.3 = (f32[128]{0:T(128)S(1)}, f32[128]{0:T(128)S(1)}, u32[]{:S(2)}, u32[]{:S(2)}) collective-permute-start(f32[128]{0:T(128)S(1)} %collective-permute-done.1), channel_id=1, source_target_pairs={{0,1},{1,2},{2,3},{3,4},{4,5},{5,6},{6,7},{7,8},{8,9},{9,10},{10,1... | collective-permute-start | bytes 1544 | tf_op jit(solution)/shard_map/ppermute | solution.py:18
  210.3 6.8 %collective-permute-start.4 = (f32[128]{0:T(128)S(1)}, f32[128]{0:T(128)S(1)}, u32[]{:S(2)}, u32[]{:S(2)}) collective-permute-start(f32[128]{0:T(128)S(1)} %collective-permute-done.2), channel_id=1, source_target_pairs={{0,15},{1,0},{2,1},{3,2},{4,3},{5,4},{6,5},{7,6},{8,7},{9,8},{10,9... | collective-permute-start | bytes 1544 | tf_op jit(solution)/shard_map/ppermute | solution.py:23
  217.1 6.9 %collective-permute-start.5 = (f32[128]{0:T(128)S(1)}, f32[128]{0:T(128)S(1)}, u32[]{:S(2)}, u32[]{:S(2)}) collective-permute-start(f32[128]{0:T(128)S(1)} %collective-permute-done.3), channel_id=1, source_target_pairs={{0,1},{1,2},{2,3},{3,4},{4,5},{5,6},{6,7},{7,8},{8,9},{9,10},{10,1... | collective-permute-start | bytes 1544 | tf_op jit(solution)/shard_map/ppermute | solution.py:18
  217.1 6.9 %collective-permute-start.6 = (f32[128]{0:T(128)S(1)}, f32[128]{0:T(128)S(1)}, u32[]{:S(2)}, u32[]{:S(2)}) collective-permute-start(f32[128]{0:T(128)S(1)} %collective-permute-done.4), channel_id=1, source_target_pairs={{0,15},{1,0},{2,1},{3,2},{4,3},{5,4},{6,5},{7,6},{8,7},{9,8},{10,9... | collective-permute-start | bytes 1544 | tf_op jit(solution)/shard_map/ppermute | solution.py:23
  223.9 6.9 %collective-permute-start.7 = (f32[128]{0:T(128)S(1)}, f32[128]{0:T(128)S(1)}, u32[]{:S(2)}, u32[]{:S(2)}) collective-permute-start(f32[128]{0:T(128)S(1)} %collective-permute-done.5), channel_id=1, source_target_pairs={{0,1},{1,2},{2,3},{3,4},{4,5},{5,6},{6,7},{7,8},{8,9},{9,10},{10,1... | collective-permute-start | bytes 1544 | tf_op jit(solution)/shard_map/ppermute | solution.py:18
  224.0 6.9 %collective-permute-start.8 = (f32[128]{0:T(128)S(1)}, f32[128]{0:T(128)S(1)}, u32[]{:S(2)}, u32[]{:S(2)}) collective-permute-start(f32[128]{0:T(128)S(1)} %collective-permute-done.6), channel_id=1, source_target_pairs={{0,15},{1,0},{2,1},{3,2},{4,3},{5,4},{6,5},{7,6},{8,7},{9,8},{10,9... | collective-permute-start | bytes 1544 | tf_op jit(solution)/shard_map/ppermute | solution.py:23
  230.8 6.9 %collective-permute-start.9 = (f32[128]{0:T(128)S(1)}, f32[128]{0:T(128)S(1)}, u32[]{:S(2)}, u32[]{:S(2)}) collective-permute-start(f32[128]{0:T(128)S(1)} %collective-permute-done.7), channel_id=1, source_target_pairs={{0,1},{1,2},{2,3},{3,4},{4,5},{5,6},{6,7},{7,8},{8,9},{9,10},{10,1... | collective-permute-start | bytes 1544 | tf_op jit(solution)/shard_map/ppermute | solution.py:18
  230.8 6.9 %collective-permute-start.10 = (f32[128]{0:T(128)S(1)}, f32[128]{0:T(128)S(1)}, u32[]{:S(2)}, u32[]{:S(2)}) collective-permute-start(f32[128]{0:T(128)S(1)} %collective-permute-done.8), channel_id=1, source_target_pairs={{0,15},{1,0},{2,1},{3,2},{4,3},{5,4},{6,5},{7,6},{8,7},{9,8},{10,9... | collective-permute-start | bytes 1544 | tf_op jit(solution)/shard_map/ppermute | solution.py:23
  237.7 6.9 %collective-permute-start.11 = (f32[128]{0:T(128)S(1)}, f32[128]{0:T(128)S(1)}, u32[]{:S(2)}, u32[]{:S(2)}) collective-permute-start(f32[128]{0:T(128)S(1)} %collective-permute-done.9), channel_id=1, source_target_pairs={{0,1},{1,2},{2,3},{3,4},{4,5},{5,6},{6,7},{7,8},{8,9},{9,10},{10,1... | collective-permute-start | bytes 1544 | tf_op jit(solution)/shard_map/ppermute | solution.py:18
  237.7 6.9 %collective-permute-start.12 = (f32[128]{0:T(128)S(1)}, f32[128]{0:T(128)S(1)}, u32[]{:S(2)}, u32[]{:S(2)}) collective-permute-start(f32[128]{0:T(128)S(1)} %collective-permute-done.10), channel_id=1, source_target_pairs={{0,15},{1,0},{2,1},{3,2},{4,3},{5,4},{6,5},{7,6},{8,7},{9,8},{10,9... | collective-permute-start | bytes 1544 | tf_op jit(solution)/shard_map/ppermute | solution.py:23
  244.5 6.9 %collective-permute-start.13 = (f32[128]{0:T(128)S(1)}, f32[128]{0:T(128)S(1)}, u32[]{:S(2)}, u32[]{:S(2)}) collective-permute-start(f32[128]{0:T(128)S(1)} %collective-permute-done.11), channel_id=1, source_target_pairs={{0,1},{1,2},{2,3},{3,4},{4,5},{5,6},{6,7},{7,8},{8,9},{9,10},{10,1... | collective-permute-start | bytes 1544 | tf_op jit(solution)/shard_map/ppermute | solution.py:18
  244.5 6.9 %collective-permute-start.14 = (f32[128]{0:T(128)S(1)}, f32[128]{0:T(128)S(1)}, u32[]{:S(2)}, u32[]{:S(2)}) collective-permute-start(f32[128]{0:T(128)S(1)} %collective-permute-done.12), channel_id=1, source_target_pairs={{0,15},{1,0},{2,1},{3,2},{4,3},{5,4},{6,5},{7,6},{8,7},{9,8},{10,9... | collective-permute-start | bytes 1544 | tf_op jit(solution)/shard_map/ppermute | solution.py:23
  251.4 6.9 %collective-permute-start.15 = (f32[128]{0:T(128)S(1)}, f32[128]{0:T(128)S(1)}, u32[]{:S(2)}, u32[]{:S(2)}) collective-permute-start(f32[128]{0:T(128)S(1)} %collective-permute-done.13), channel_id=1, source_target_pairs={{0,1},{1,2},{2,3},{3,4},{4,5},{5,6},{6,7},{7,8},{8,9},{9,10},{10,1... | collective-permute-start | bytes 1544 | tf_op jit(solution)/shard_map/ppermute | solution.py:18
  258.3 3.2 %copy-start.4 = (f32[1,2048]{1,0:T(1,128)}, f32[1,2048]{1,0:T(1,128)S(1)}, u32[]{:S(2)}) copy-start(f32[1,2048]{1,0:T(1,128)S(1)} %constant_dynamic-update-slice_fusion) | copy-start | bytes 24580
Sparse Core Ops, SparseCore 0:
  10.2 92.5 all-gather.2
  106.3 94.2 reduce-scatter.1
